TPU v7x, 32 devices: a whole 2x2x4 slice. The times are simulated.
32 devices in a mesh: geom: 2 (over x), op: 8 (over z, y), col: 2 (over core).
Axes of the slice: x: 2, y: 2, z: 4, core: 2. Of those that a mesh axis runs over, the one named last changes fastest.
Arguments:
- wave_coef: float32 [2048, 1024], P('geom', 'col'), parts along dimension 0, may hold values from -6 to 6
- diag_energy: float32 [2048, 1024], P('geom', 'col'), parts along dimension 0, may hold values from -4 to 4
- left_block: bfloat16 [32, 1024, 1024], P(('geom', 'op')), parts along dimension 0, may hold values from -0.1875 to 0.1875
- right_block: bfloat16 [32, 1024, 1024], P(('geom', 'op'), None, 'col'), parts along dimension 0, may hold values from -0.1875 to 0.1875
- block_mask: int32 [32, 8, 8], P(('geom', 'op')), parts along dimension 0, may hold values 0 or 1
Outputs:
- new_wave: float32 [2048, 1024], P('geom', 'col'), parts along dimension 0
There are 2 independent parts, one for each index of `geom`. A program takes and returns all parts, laid end to end along the dimension named above; each array names one. Nothing has to cross between parts.
All inputs are finite; a program needn't handle non-finite values. No bound on the sum of `block_mask` on one device may be relied on, other than what follows from the above.
Results may differ from a plain program's by a relative error of at most 0.0042.
The roundings to bfloat16 on the way count: a program that leaves them out, or rounds other values in their place, can miss the bound.
Values may be sent and summed in bfloat16 or wider, within the bound.
A program may use at most 64 MiB of HBM per device.

v0:
```python
import jax
import jax.numpy as jnp
from jax import lax
from jax.sharding import PartitionSpec as P

M = 1024
STEPS = 2


def apply_mask(left_block, block_mask):
    total, width, _ = left_block.shape
    blocks = block_mask.shape[1]
    inside = width // blocks
    grid = left_block.reshape(total, blocks, inside, blocks, inside)
    keep = block_mask.astype(jnp.bfloat16)[:, :, None, :, None]
    return (grid * keep).reshape(total, width, width)


def correct(coef, sigma, diag_energy, correlation, weight, cells):
    theta = correlation / cells / (weight / cells + 1e-06)
    spacing = diag_energy - theta
    correction = (sigma - theta * coef) * spacing / jnp.maximum(spacing * spacing, 1.0)
    return coef - correction


def update_cols(coef, sigma, diag_energy, cells):
    correlation, weight = lax.psum((jnp.sum(coef * sigma), jnp.sum(coef * coef)), "col")
    moved = correct(coef, sigma, diag_energy, correlation, weight, cells)
    norm_sum = lax.psum(jnp.sum(moved * moved), "col")
    return moved * lax.rsqrt(norm_sum / cells + 1e-06)


def local(wave_coef, diag_energy, left_block, right_block, block_mask):
    masked = apply_mask(left_block, block_mask)
    cells = float(M * M)
    coef = wave_coef
    wave = wave_coef.astype(jnp.bfloat16)
    for step in range(STEPS):
        wave = coef.astype(jnp.bfloat16)
        inner = jnp.einsum(
            "mj,kjc->kmc",
            lax.all_gather(wave, "col", axis=1, tiled=True),
            right_block,
            preferred_element_type=jnp.float32,
        ).astype(jnp.bfloat16)
        partial_sum = jnp.einsum("kab,kbc->ac", masked, inner, preferred_element_type=jnp.float32)
        sigma = lax.psum(partial_sum, "op")
        coef = update_cols(coef, sigma, diag_energy, cells)
    return coef


def solution(mesh):
    in_specs = (
        P("geom", "col"),
        P("geom", "col"),
        P(("geom", "op"), None, None),
        P(("geom", "op"), None, "col"),
        P(("geom", "op"), None, None),
    )
    out_specs = P("geom", "col")
    return jax.shard_map(local, mesh=mesh, in_specs=in_specs, out_specs=out_specs, check_vma=False)
```

profile of v0, /device:TPU:0, one launch (start us, length us, event | category | flops | bytes accessed | tf_op | source)
XLA Modules:
  0.0 310.1 jit_solution(6017176165767036142)
XLA Ops:
  6.5 0.0 copy-start
  6.5 0.0 copy-start.1
  6.5 0.0 all-gather.3.cloned.1.call-start
  6.5 2.9 convert_element_type.22
  9.4 0.0 all-gather.3.cloned.1.call-update
  9.4 0.0 all-reduce.5.cloned.1.call-start
  9.5 0.0 copy-done.1
  9.5 2.5 mul.65
  12.0 7.4 %mul.66 = bf16[2,1024,1024]{2,1,0:T(8,128)(2,1)} reshape(bf16[2,8,128,8,128]{4,3,2,1,0:T(8,128)(2,1)} %mul.65) | data formatting | bytes 8388608 | tf_op jit(solution)/shard_map/mul | solution.py:16
  19.4 8.1 %mul.67 = bf16[2,1024,1024]{2,1,0:T(8,128)(2,1)} multiply(bf16[2,1024,1024]{2,1,0:T(8,128)(2,1)} %param.7, bf16[2,1024,1024]{2,1,0:T(8,128)(2,1)} %mul.66) | non-fusion elementwise | flops 2097152 | bytes 12582912 | tf_op jit(solution)/shard_map/mul | solution.py:16
  27.5 0.0 all-gather.3.cloned.1.call-done
  27.5 0.0 copy-done
  27.5 8.7 %fusion.10 = f32[1024,512]{1,0:T(8,128)} fusion(bf16[2,1024,1024]{2,1,0:T(8,128)(2,1)} %mul.67, bf16[2,1024,512]{2,1,0:T(8,128)(2,1)S(1)} %copy-done, bf16[1024,1024]{1,0:T(8,128)(2,1)} %all-gather.3.cloned.1.call-done), kind=kOutput, calls=%fused_computation.19 | convolution fusion | flops 4296015872 | bytes 10485760 | tf_op jit(solution)/shard_map/kab,kbc->ac/dot_general | solution.py:46
  36.1 0.0 all-reduce.5.cloned.1.call-update
  36.2 0.0 all-gather.5.cloned.1.call-start
  36.2 104.7 %all-reduce.5.cloned.1.call-done = f32[1024,512]{1,0:T(8,128)} async-done(((f32[1024,512]{1,0:T(8,128)}), f32[1024,512]{1,0:T(8,128)}) %all-reduce.5.cloned.1.call-update) | async-done | bytes 2097168 | tf_op jit(solution)/shard_map/psum | solution.py:47
  140.9 3.4 %multiply_reduce_fusion.4 = (f32[]{:T(128)}, f32[]{:T(128)}) fusion(f32[1024,512]{1,0:T(8,128)} %param.5, f32[1024,512]{1,0:T(8,128)} %all-reduce.5.cloned.1.call-done), kind=kLoop, calls=%fused_computation.15 | loop fusion | flops 2097150 | bytes 4194312 | tf_op jit(solution)/shard_map/reduce_sum | solution.py:27
  144.3 3.1 %all-reduce.1 = (f32[]{:T(128)}, f32[]{:T(128)}) all-reduce(f32[]{:T(128)} %get-tuple-element.8, f32[]{:T(128)} %get-tuple-element.7), channel_id=1, replica_groups=mesh['geom'=2,'op'=8,'col'=2] {'col'}, use_global_device_ids=true, to_apply=%region_2.0 | all-reduce | flops 2 | bytes 16 | tf_op jit(solution)/shard_map/psum | solution.py:27
  148.7 5.6 %multiply_reduce_fusion.3 = (f32[]{:T(128)}, f32[1024,512]{1,0:T(8,128)}) fusion(f32[1024,512]{1,0:T(8,128)} %param.5, f32[1024,512]{1,0:T(8,128)} %param.6, f32[1024,512]{1,0:T(8,128)} %all-reduce.5.cloned.1.call-done, f32[]{:T(128)S(6)} %div.32), kind=kLoop, calls=%fused_computation.13 | loop fusion | flops 5242879 | bytes 8388616 | tf_op jit(solution)/shard_map/reduce_sum | solution.py:29
  154.3 3.1 %psum.59 = f32[]{:T(128)} all-reduce(f32[]{:T(128)} %get-tuple-element.15), channel_id=1, replica_groups=mesh['geom'=2,'op'=8,'col'=2] {'col'}, use_global_device_ids=true, to_apply=%region_6.0 | all-reduce | flops 1 | bytes 8 | tf_op jit(solution)/shard_map/psum | solution.py:29
  158.1 2.8 multiply_convert_fusion
  160.9 0.0 all-gather.5.cloned.1.call-update
  160.9 0.0 all-reduce.7.cloned.1.call-start
  161.0 10.0 %all-gather.5.cloned.1.call-done = bf16[1024,1024]{1,0:T(8,128)(2,1)} async-done(((bf16[1024,512]{1,0:T(8,128)(2,1)}), bf16[1024,1024]{1,0:T(8,128)(2,1)}) %all-gather.5.cloned.1.call-update) | async-done | bytes 2097168 | tf_op jit(solution)/shard_map/all_gather | solution.py:42
  170.9 8.6 %fusion.13 = f32[1024,512]{1,0:T(8,128)} fusion(bf16[2,1024,1024]{2,1,0:T(8,128)(2,1)} %mul.67, bf16[2,1024,512]{2,1,0:T(8,128)(2,1)S(1)} %copy-done, bf16[1024,1024]{1,0:T(8,128)(2,1)} %all-gather.5.cloned.1.call-done), kind=kOutput, calls=%fused_computation.20 | convolution fusion | flops 4296015872 | bytes 10485760 | tf_op jit(solution)/shard_map/kab,kbc->ac/dot_general | solution.py:46
  179.6 0.0 all-reduce.7.cloned.1.call-update
  179.6 103.6 %all-reduce.7.cloned.1.call-done = f32[1024,512]{1,0:T(8,128)} async-done(((f32[1024,512]{1,0:T(8,128)}), f32[1024,512]{1,0:T(8,128)}) %all-reduce.7.cloned.1.call-update) | async-done | bytes 2097168 | tf_op jit(solution)/shard_map/psum | solution.py:47
  283.2 3.4 %multiply_reduce_fusion.1 = (f32[]{:T(128)}, f32[]{:T(128)}) fusion(f32[1024,512]{1,0:T(8,128)} %get-tuple-element.16, f32[]{:T(128)S(6)} %rsqrt.6, f32[1024,512]{1,0:T(8,128)} %all-reduce.7.cloned.1.call-done), kind=kLoop, calls=%fused_computation.10 | loop fusion | flops 2621438 | bytes 4194316 | tf_op jit(solution)/shard_map/reduce_sum | solution.py:27
  286.6 3.1 all-reduce
  290.9 5.6 %multiply_reduce_fusion = (f32[]{:T(128)}, f32[1024,512]{1,0:T(8,128)}) fusion(f32[1024,512]{1,0:T(8,128)} %param.6, f32[1024,512]{1,0:T(8,128)} %all-reduce.7.cloned.1.call-done, f32[]{:T(128)S(6)} %div.37, f32[1024,512]{1,0:T(8,128)} %get-tuple-element.16, f32[]{:T(128)S(6)} %rsqrt.6), kind=kLoop, calls=%fused_computation.8 | loop fusion | flops 5767167 | bytes 8388620 | tf_op jit(solution)/shard_map/reduce_sum | solution.py:29
  296.5 3.2 %psum.63 = f32[]{:T(128)} all-reduce(f32[]{:T(128)} %get-tuple-element.13), channel_id=1, replica_groups=mesh['geom'=2,'op'=8,'col'=2] {'col'}, use_global_device_ids=true, to_apply=%region_13.0 | all-reduce | flops 1 | bytes 8 | tf_op jit(solution)/shard_map/psum | solution.py:29
  300.4 3.1 %broadcast_multiply_fusion = f32[1024,512]{1,0:T(8,128)} fusion(f32[1024,512]{1,0:T(8,128)} %get-tuple-element.14, f32[]{:T(128)S(6)} %rsqrt.7), kind=kLoop, calls=%fused_computation.21 | loop fusion | flops 524288 | bytes 4194308 | tf_op jit(solution)/shard_map/mul | solution.py:30
  (1 shorter events, 0.0 us)
Async XLA Ops:
  6.5 20.9 %copy-start = (bf16[2,1024,512]{2,1,0:T(8,128)(2,1)S(1)}, bf16[2,1024,512]{2,1,0:T(8,128)(2,1)}, u32[]{:S(2)}) copy-start(bf16[2,1024,512]{2,1,0:T(8,128)(2,1)} %param.8) | copy-start | bytes 6291460
  6.5 2.9 copy-start.1
  6.5 20.9 %all-gather.3.cloned.1.call-start = ((), (), s32[]{:S(2)}) async-start(), calls=%async_computation | async-start | bytes 3145728 | tf_op jit(solution)/shard_map/all_gather | solution.py:42
  9.4 131.5 %all-reduce.5.cloned.1.call-start = ((), (), s32[]{:S(2)}) async-start(), calls=%async_computation.1 | async-start | bytes 4194304 | tf_op jit(solution)/shard_map/psum | solution.py:47
  36.2 134.8 %all-gather.5.cloned.1.call-start = ((), (), s32[]{:S(2)}) async-start(), calls=%async_computation.2 | async-start | bytes 3145728 | tf_op jit(solution)/shard_map/all_gather | solution.py:42
  160.9 122.3 %all-reduce.7.cloned.1.call-start = ((), (), s32[]{:S(2)}) async-start(), calls=%async_computation.3 | async-start | bytes 4194304 | tf_op jit(solution)/shard_map/psum | solution.py:47
Sparse Core Ops, SparseCore 0:
  9.5 13.2 all-gather.2
  36.3 104.5 all-reduce.4
  161.0 9.8 all-gather.4
  179.7 103.4 all-reduce.6
where the time goes:
time: 311 us; the launch traced here: 310 us
  waiting for transfers between devices  218 us (70%)
  other arithmetic  34.9 us (11%)
  matrix products  17.3 us (6%)
  between operations  17 us (5%)
  blocking collectives  12.5 us (4%)
  local copies, waits for them, and re-layouts  9.93 us (3%)
    psum x2, waiting for transfers between devices, local(): sigma = lax.psum(partial_sum, 'op')  208 us
    dot_general x2, matrix products, local(): jnp.einsum('kab,kbc->ac', masked, inner, preferred_element_type=jnp.float32)  17.3 us
    reduce_sum x2, other arithmetic, update_cols(): norm_sum = lax.psum(jnp.sum(moved * moved), 'col')  11.2 us
    all_gather x2, waiting for transfers between devices, local(): lax.all_gather(wave, 'col', axis=1, tiled=True)  9.96 us
    mul x2, local copies, waits for them, and re-layouts, apply_mask(): return (grid * keep).reshape(total, width, width)  9.92 us
    mul x1, other arithmetic, apply_mask(): return (grid * keep).reshape(total, width, width)  8.05 us
    reduce_sum x2, other arithmetic, update_cols(): jnp.sum(coef * coef)  6.78 us
    psum x2, blocking collectives, update_cols(): norm_sum = lax.psum(jnp.sum(moved * moved), 'col')  6.27 us
  transfers between devices with their start and end apart: 4, of which 3 were waited for; matrix products, arithmetic and copies ran while one was open for 6% of the time, Pallas kernels for 0%

commit v1 on v0

--- a/solution.py
+++ b/solution.py
@@ -44,7 +44,9 @@
             preferred_element_type=jnp.float32,
         ).astype(jnp.bfloat16)
         partial_sum = jnp.einsum("kab,kbc->ac", masked, inner, preferred_element_type=jnp.float32)
-        sigma = lax.psum(partial_sum, "op")
+        sigma = partial_sum
+        for hop in (1, 2, 4):
+            sigma = sigma + lax.ppermute(sigma, "op", [(dev, dev ^ hop) for dev in range(8)])
         coef = update_cols(coef, sigma, diag_energy, cells)
     return coef
 

time: 311 us -> 483 us (1.55)
  waiting for transfers between devices: 218 us -> 373 us
  starting transfers between devices: 0.13 us -> 13.7 us
    ppermute x0 -> x6, waiting for transfers between devices: none -> 361 us  [local(): lax.ppermute(sigma, 'op', [(dev, dev ^ hop) for dev in range(8)])]
    psum x2 -> x0, waiting for transfers between devices: 208 us -> none  [local(): sigma = lax.psum(partial_sum, 'op')]
    ppermute x0 -> x6, starting transfers between devices: none -> 13.6 us  [local(): lax.ppermute(sigma, 'op', [(dev, dev ^ hop) for dev in range(8)])]
    add x0 -> x4, other arithmetic: none -> 5.09 us  [local(): sigma + lax.ppermute(sigma, 'op', [(dev, dev ^ hop) for dev in range(8)])]
  transfers between devices with their start and end apart: 4 -> 8, of which waited for: 3 -> 7; matrix products, arithmetic and copies ran while one was open for 6% -> 4% of each run, Pallas kernels for 0% -> 0%
where the time goes in v1:
time: 483 us; the launch traced here: 482 us
  waiting for transfers between devices  373 us (77%)
  other arithmetic  38.6 us (8%)
  matrix products  17.3 us (4%)
  between operations  17.3 us (4%)
  starting transfers between devices  13.7 us (3%)
  blocking collectives  12.6 us (3%)
  local copies, waits for them, and re-layouts  9.94 us (2%)
    ppermute x6, waiting for transfers between devices, local(): lax.ppermute(sigma, 'op', [(dev, dev ^ hop) for dev in range(8)])  361 us
    dot_general x2, matrix products, local(): jnp.einsum('kab,kbc->ac', masked, inner, preferred_element_type=jnp.float32)  17.3 us
    ppermute x6, starting transfers between devices, local(): lax.ppermute(sigma, 'op', [(dev, dev ^ hop) for dev in range(8)])  13.6 us
    all_gather x2, waiting for transfers between devices, local(): lax.all_gather(wave, 'col', axis=1, tiled=True)  11.7 us
    reduce_sum x2, other arithmetic, update_cols(): norm_sum = lax.psum(jnp.sum(moved * moved), 'col')  11.3 us
    mul x2, local copies, waits for them, and re-layouts, apply_mask(): return (grid * keep).reshape(total, width, width)  9.92 us
  transfers between devices with their start and end apart: 8, of which 7 were waited for; matrix products, arithmetic and copies ran while one was open for 4% of the time, Pallas kernels for 0%

profile of v1, /device:TPU:0, one launch (start us, length us, event | category | flops | bytes accessed | tf_op | source)
XLA Modules:
  0.0 482.3 jit_solution(18027222087053127046)
XLA Ops:
  6.5 0.0 copy-start
  6.5 0.0 copy-start.3
  6.5 0.0 all-gather.3.cloned.1.call-start
  6.5 2.9 convert_element_type.22
  9.4 0.0 all-gather.3.cloned.1.call-update
  9.4 0.0 all-gather.5.cloned.1.call-start
  9.5 0.0 copy-done.3
  9.5 2.5 mul.65
  12.0 7.4 %mul.66 = bf16[2,1024,1024]{2,1,0:T(8,128)(2,1)} reshape(bf16[2,8,128,8,128]{4,3,2,1,0:T(8,128)(2,1)} %mul.65) | data formatting | bytes 8388608 | tf_op jit(solution)/shard_map/mul | solution.py:16
  19.4 8.1 %mul.67 = bf16[2,1024,1024]{2,1,0:T(8,128)(2,1)} multiply(bf16[2,1024,1024]{2,1,0:T(8,128)(2,1)} %param.7, bf16[2,1024,1024]{2,1,0:T(8,128)(2,1)} %mul.66) | non-fusion elementwise | flops 2097152 | bytes 12582912 | tf_op jit(solution)/shard_map/mul | solution.py:16
  27.5 0.0 all-gather.3.cloned.1.call-done
  27.5 0.0 copy-done
  27.5 8.7 %fusion.10 = f32[1024,512]{1,0:T(8,128)} fusion(bf16[2,1024,1024]{2,1,0:T(8,128)(2,1)} %mul.67, bf16[2,1024,512]{2,1,0:T(8,128)(2,1)S(1)} %copy-done, bf16[1024,1024]{1,0:T(8,128)(2,1)} %all-gather.3.cloned.1.call-done), kind=kOutput, calls=%fused_computation.19 | convolution fusion | flops 4296015872 | bytes 10485760 | tf_op jit(solution)/shard_map/kab,kbc->ac/dot_general | solution.py:46
  36.1 2.7 collective-permute-start
  38.9 45.9 %collective-permute-done = f32[1024,512]{1,0:T(8,128)S(1)} collective-permute-done((f32[1024,512]{1,0:T(8,128)}, f32[1024,512]{1,0:T(8,128)S(1)}, u32[]{:S(2)}, u32[]{:S(2)}) %collective-permute-start) | collective-permute-done | bytes 2097184 | tf_op jit(solution)/shard_map/ppermute | solution.py:49
  84.8 2.1 add.42
  86.9 0.0 copy-start.2
  86.9 1.9 collective-permute-start.1
  88.7 45.1 %collective-permute-done.1 = f32[1024,512]{1,0:T(8,128)S(1)} collective-permute-done((f32[1024,512]{1,0:T(8,128)S(1)}, f32[1024,512]{1,0:T(8,128)S(1)}, u32[]{:S(2)}, u32[]{:S(2)}) %collective-permute-start.1) | collective-permute-done | bytes 2097184 | tf_op jit(solution)/shard_map/ppermute | solution.py:49
  133.8 0.5 add.43
  134.3 2.7 collective-permute-start.2
  137.1 89.2 %collective-permute-done.2 = f32[1024,512]{1,0:T(8,128)S(1)} collective-permute-done((f32[1024,512]{1,0:T(8,128)S(1)}, f32[1024,512]{1,0:T(8,128)S(1)}, u32[]{:S(2)}, u32[]{:S(2)}) %collective-permute-start.2) | collective-permute-done | bytes 2097184 | tf_op jit(solution)/shard_map/ppermute | solution.py:49
  226.3 0.0 copy-done.2
  226.3 2.7 multiply_reduce_fusion.4
  228.9 3.1 all-reduce.1
  233.4 5.7 %multiply_reduce_fusion.3 = (f32[]{:T(128)}, f32[1024,512]{1,0:T(8,128)}) fusion(f32[1024,512]{1,0:T(8,128)} %param.5, f32[1024,512]{1,0:T(8,128)} %param.6, f32[1024,512]{1,0:T(8,128)} %get-tuple-element.18, f32[]{:T(128)S(6)} %div.32), kind=kLoop, calls=%fused_computation.13 | loop fusion | flops 5242879 | bytes 8388616 | tf_op jit(solution)/shard_map/reduce_sum | solution.py:29
  239.0 3.3 psum.44
  242.9 2.8 multiply_convert_fusion
  245.7 0.0 all-gather.5.cloned.1.call-update
  245.8 11.7 %all-gather.5.cloned.1.call-done = bf16[1024,1024]{1,0:T(8,128)(2,1)} async-done(((bf16[1024,512]{1,0:T(8,128)(2,1)}), bf16[1024,1024]{1,0:T(8,128)(2,1)}) %all-gather.5.cloned.1.call-update) | async-done | bytes 2097168 | tf_op jit(solution)/shard_map/all_gather | solution.py:42
  257.5 8.6 %fusion.13 = f32[1024,512]{1,0:T(8,128)} fusion(bf16[2,1024,1024]{2,1,0:T(8,128)(2,1)} %mul.67, bf16[2,1024,512]{2,1,0:T(8,128)(2,1)S(1)} %copy-done, bf16[1024,1024]{1,0:T(8,128)(2,1)} %all-gather.5.cloned.1.call-done), kind=kOutput, calls=%fused_computation.20 | convolution fusion | flops 4296015872 | bytes 10485760 | tf_op jit(solution)/shard_map/kab,kbc->ac/dot_general | solution.py:46
  266.1 1.7 collective-permute-start.3
  267.9 46.3 %collective-permute-done.3 = f32[1024,512]{1,0:T(8,128)S(1)} collective-permute-done((f32[1024,512]{1,0:T(8,128)}, f32[1024,512]{1,0:T(8,128)S(1)}, u32[]{:S(2)}, u32[]{:S(2)}) %collective-permute-start.3) | collective-permute-done | bytes 2097184 | tf_op jit(solution)/shard_map/ppermute | solution.py:49
  314.2 2.1 add.47
  316.2 0.0 copy-start.1
  316.2 1.8 collective-permute-start.4
  318.1 45.2 %collective-permute-done.4 = f32[1024,512]{1,0:T(8,128)S(1)} collective-permute-done((f32[1024,512]{1,0:T(8,128)S(1)}, f32[1024,512]{1,0:T(8,128)S(1)}, u32[]{:S(2)}, u32[]{:S(2)}) %collective-permute-start.4) | collective-permute-done | bytes 2097184 | tf_op jit(solution)/shard_map/ppermute | solution.py:49
  363.3 0.5 add.48
  363.8 2.7 collective-permute-start.5
  366.5 89.3 %collective-permute-done.5 = f32[1024,512]{1,0:T(8,128)S(1)} collective-permute-done((f32[1024,512]{1,0:T(8,128)S(1)}, f32[1024,512]{1,0:T(8,128)S(1)}, u32[]{:S(2)}, u32[]{:S(2)}) %collective-permute-start.5) | collective-permute-done | bytes 2097184 | tf_op jit(solution)/shard_map/ppermute | solution.py:49
  455.8 0.0 copy-done.1
  455.8 2.7 multiply_reduce_fusion.1
  458.5 3.1 all-reduce
  462.8 5.6 %multiply_reduce_fusion = (f32[]{:T(128)}, f32[1024,512]{1,0:T(8,128)}) fusion(f32[1024,512]{1,0:T(8,128)} %param.6, f32[1024,512]{1,0:T(8,128)} %get-tuple-element.15, f32[]{:T(128)S(6)} %div.37, f32[1024,512]{1,0:T(8,128)} %get-tuple-element.17, f32[]{:T(128)S(6)} %rsqrt.6), kind=kLoop, calls=%fused_computation.8 | loop fusion | flops 5767167 | bytes 8388620 | tf_op jit(solution)/shard_map/reduce_sum | solution.py:29
  468.4 3.2 psum.47
  472.3 3.1 broadcast_multiply_fusion
  (1 shorter events, 0.0 us)
Async XLA Ops:
  6.5 20.9 %copy-start = (bf16[2,1024,512]{2,1,0:T(8,128)(2,1)S(1)}, bf16[2,1024,512]{2,1,0:T(8,128)(2,1)}, u32[]{:S(2)}) copy-start(bf16[2,1024,512]{2,1,0:T(8,128)(2,1)} %param.8) | copy-start | bytes 6291460
  6.5 2.9 copy-start.3
  6.5 20.9 %all-gather.3.cloned.1.call-start = ((), (), s32[]{:S(2)}) async-start(), calls=%async_computation | async-start | bytes 3145728 | tf_op jit(solution)/shard_map/all_gather | solution.py:42
  9.4 248.1 %all-gather.5.cloned.1.call-start = ((), (), s32[]{:S(2)}) async-start(), calls=%async_computation.1 | async-start | bytes 3145728 | tf_op jit(solution)/shard_map/all_gather | solution.py:42
  36.1 48.7 %collective-permute-start = (f32[1024,512]{1,0:T(8,128)}, f32[1024,512]{1,0:T(8,128)S(1)}, u32[]{:S(2)}, u32[]{:S(2)}) collective-permute-start(f32[1024,512]{1,0:T(8,128)} %fusion.10), channel_id=1, source_target_pairs={{0,2},{2,0},{4,6},{6,4},{8,10},{10,8},{12,14},{14,12},{1,3},{3,1},... | collective-permute-start | bytes 6291464 | tf_op jit(solution)/shard_map/ppermute | solution.py:49
  86.9 139.4 %copy-start.2 = (f32[1024,512]{1,0:T(8,128)S(1)}, f32[1024,512]{1,0:T(8,128)}, u32[]{:S(2)}) copy-start(f32[1024,512]{1,0:T(8,128)} %param.5) | copy-start | bytes 6291460
  86.9 47.0 %collective-permute-start.1 = (f32[1024,512]{1,0:T(8,128)S(1)}, f32[1024,512]{1,0:T(8,128)S(1)}, u32[]{:S(2)}, u32[]{:S(2)}) collective-permute-start(f32[1024,512]{1,0:T(8,128)S(1)} %add.42), channel_id=1, source_target_pairs={{0,4},{2,6},{4,0},{6,2},{8,12},{10,14},{12,8},{14,10},{1,5},{3,7},... | collective-permute-start | bytes 6291464 | tf_op jit(solution)/shard_map/ppermute | solution.py:49
  134.3 91.9 %collective-permute-start.2 = (f32[1024,512]{1,0:T(8,128)S(1)}, f32[1024,512]{1,0:T(8,128)S(1)}, u32[]{:S(2)}, u32[]{:S(2)}) collective-permute-start(f32[1024,512]{1,0:T(8,128)S(1)} %add.43), channel_id=1, source_target_pairs={{0,8},{2,10},{4,12},{6,14},{8,0},{10,2},{12,4},{14,6},{1,9},{3,11}... | collective-permute-start | bytes 6291464 | tf_op jit(solution)/shard_map/ppermute | solution.py:49
  266.1 48.0 %collective-permute-start.3 = (f32[1024,512]{1,0:T(8,128)}, f32[1024,512]{1,0:T(8,128)S(1)}, u32[]{:S(2)}, u32[]{:S(2)}) collective-permute-start(f32[1024,512]{1,0:T(8,128)} %fusion.13), channel_id=1, source_target_pairs={{0,2},{2,0},{4,6},{6,4},{8,10},{10,8},{12,14},{14,12},{1,3},{3,1},... | collective-permute-start | bytes 6291464 | tf_op jit(solution)/shard_map/ppermute | solution.py:49
  316.2 139.6 %copy-start.1 = (f32[1024,512]{1,0:T(8,128)S(1)}, f32[1024,512]{1,0:T(8,128)}, u32[]{:S(2)}) copy-start(f32[1024,512]{1,0:T(8,128)} %get-tuple-element.17) | copy-start | bytes 6291460
  316.2 47.1 %collective-permute-start.4 = (f32[1024,512]{1,0:T(8,128)S(1)}, f32[1024,512]{1,0:T(8,128)S(1)}, u32[]{:S(2)}, u32[]{:S(2)}) collective-permute-start(f32[1024,512]{1,0:T(8,128)S(1)} %add.47), channel_id=1, source_target_pairs={{0,4},{2,6},{4,0},{6,2},{8,12},{10,14},{12,8},{14,10},{1,5},{3,7},... | collective-permute-start | bytes 6291464 | tf_op jit(solution)/shard_map/ppermute | solution.py:49
  363.8 92.0 %collective-permute-start.5 = (f32[1024,512]{1,0:T(8,128)S(1)}, f32[1024,512]{1,0:T(8,128)S(1)}, u32[]{:S(2)}, u32[]{:S(2)}) collective-permute-start(f32[1024,512]{1,0:T(8,128)S(1)} %add.48), channel_id=1, source_target_pairs={{0,8},{2,10},{4,12},{6,14},{8,0},{10,2},{12,4},{14,6},{1,9},{3,11}... | collective-permute-start | bytes 6291464 | tf_op jit(solution)/shard_map/ppermute | solution.py:49
Sparse Core Ops, SparseCore 0:
  9.5 13.2 all-gather.2
  245.9 11.5 all-gather.4
